TPU v7x, 128 devices: a whole 4x4x4 slice. The times are simulated.
128 devices in a mesh: row: 16 (over z, x), mp: 8 (over y, core).
Axes of the slice: x: 4, y: 4, z: 4, core: 2. Of those that a mesh axis runs over, the one named last changes fastest.
Arguments:
- token_ids: int32 [128, 128], P('row'), may hold values from 0 to 511
- set_lengths: int32 [128], P('row'), may hold values from 32 to 128
- live_counts: int32 [16], replicated, may hold values from 1 to 8, 64 in all
- embed_table: bfloat16 [512, 5120], replicated, may hold values from -3 to 3
- position_table: bfloat16 [128, 5120], replicated, may hold values from -3 to 3
- norm_gain: float32 [5120], replicated, may hold values from 0.1 to 1.9
- w_query: bfloat16 [5120, 5120], P('row', 'mp')
- w_key: bfloat16 [5120, 5120], P('row', 'mp')
- w_value: bfloat16 [5120, 5120], P('row', 'mp'), may hold values from -0.078125 to 0.078125
- w_out: bfloat16 [5120, 5120], P('mp', 'row'), may hold values from -0.078125 to 0.078125
Outputs:
- verified: bfloat16 [128, 128, 5120], P('row', None, 'mp')
Inputs may be any that keep to these rules, and one draw needn't show every extreme that they name: Owner group g has live_counts[g] live sets, its first slots; the counts sum to 64 and one group holds 8. `set_lengths`: positions at or past a set's length are padding.
All inputs are finite; a program needn't handle non-finite values.
Results may differ from a plain program's by a relative error of at most 0.017.
Values may be sent and summed in bfloat16 or wider, within the bound.
No kernel may reach another device: no remote copies, remote signals or barrier semaphores. Data moves between devices by JAX's collectives and lax.ppermute only.
A program may use at most 128 MiB of HBM per device.

v0:
```python
import jax
import jax.numpy as jnp
from jax import lax
from jax.sharding import PartitionSpec as P

DH = 128


def prepare(group_ids, embed_table, position_table, norm_gain):
    summed = (
        jnp.take(embed_table, group_ids, axis=0).astype(jnp.float32)
        + position_table.astype(jnp.float32)[None]
    )
    stored = lax.optimization_barrier(summed.astype(jnp.bfloat16))
    widened = stored.astype(jnp.float32)
    inverse = lax.rsqrt(jnp.mean(widened * widened, axis=-1, keepdims=True) + 1e-05)
    normed = (widened * inverse * norm_gain).astype(jnp.bfloat16)
    return (stored, normed)


def attend(query, keys, values, group_lengths):
    set_count = group_lengths.shape[0]
    seq_len = query.shape[0] // set_count
    q_four = query.reshape(set_count, seq_len, -1, DH)
    k_four = keys.reshape(set_count, seq_len, -1, DH)
    v_four = values.reshape(set_count, seq_len, -1, DH)
    scores = jnp.einsum(
        "sqhd,skhd->shqk", q_four, k_four, preferred_element_type=jnp.float32
    ) * DH ** (-0.5)
    valid = jnp.arange(seq_len)[None, :] < group_lengths[:, None]
    scores = jnp.where(valid[:, None, None, :], scores, -1e30)
    highest = jnp.max(scores, axis=-1, keepdims=True)
    expo = jnp.exp(scores - highest)
    weights = (expo / jnp.sum(expo, axis=-1, keepdims=True)).astype(jnp.bfloat16)
    mixed = jnp.einsum("shqk,skhd->sqhd", weights, v_four, preferred_element_type=jnp.float32)
    return mixed.astype(jnp.bfloat16).reshape(set_count * seq_len, -1)


def verify(
    group_ids,
    group_lengths,
    live,
    embed_table,
    position_table,
    norm_gain,
    w_query,
    w_key,
    w_value,
    w_out,
):
    set_count, seq_len = group_ids.shape
    stored, normed = prepare(group_ids, embed_table, position_table, norm_gain)
    flat = normed.reshape(set_count * seq_len, -1)
    query = jnp.dot(
        flat, lax.all_gather(w_query, "row", axis=0, tiled=True), preferred_element_type=jnp.float32
    )
    keys = jnp.dot(
        flat, lax.all_gather(w_key, "row", axis=0, tiled=True), preferred_element_type=jnp.float32
    )
    values = jnp.dot(
        flat, lax.all_gather(w_value, "row", axis=0, tiled=True), preferred_element_type=jnp.float32
    )
    mixed = attend(
        query.astype(jnp.bfloat16),
        keys.astype(jnp.bfloat16),
        values.astype(jnp.bfloat16),
        group_lengths,
    )
    partial_value = jnp.dot(
        mixed, lax.all_gather(w_out, "row", axis=1, tiled=True), preferred_element_type=jnp.float32
    )
    summed = lax.psum_scatter(
        partial_value.astype(jnp.bfloat16), "mp", scatter_dimension=1, tiled=True
    ).astype(jnp.float32)
    features = summed.shape[1]
    residual = lax.dynamic_slice_in_dim(
        stored.reshape(set_count * seq_len, -1), lax.axis_index("mp") * features, features, 1
    )
    valid = jnp.arange(seq_len)[None, :] < group_lengths[:, None]
    keep = (live[:, None] & valid).reshape(-1, 1).astype(jnp.float32)
    output = ((residual.astype(jnp.float32) + summed) * keep).astype(jnp.bfloat16)
    return output.reshape(set_count, seq_len, features)


def on_device(
    token_ids,
    set_lengths,
    live_counts,
    embed_table,
    position_table,
    norm_gain,
    w_query,
    w_key,
    w_value,
    w_out,
):
    slot_count, seq_len = token_ids.shape
    my_group = lax.axis_index("row")
    own_live = jnp.arange(slot_count) < live_counts[my_group]
    return verify(
        token_ids,
        set_lengths,
        own_live,
        embed_table,
        position_table,
        norm_gain,
        w_query,
        w_key,
        w_value,
        w_out,
    )


def solution(mesh):
    in_specs = (
        P("row", None),
        P("row"),
        P(),
        P(),
        P(),
        P(),
        P("row", "mp"),
        P("row", "mp"),
        P("row", "mp"),
        P("mp", "row"),
    )
    out_specs = P("row", None, "mp")
    return jax.shard_map(
        on_device, mesh=mesh, in_specs=in_specs, out_specs=out_specs, check_vma=False
    )
```

profile of v0, /device:TPU:1, one launch (start us, length us, event | category | flops | bytes accessed | tf_op | source)
XLA Modules:
  0.0 368.8 jit_solution(6773406523633156874)
XLA Ops:
  6.5 0.7 all-gather.7.cloned.1.call-update
  7.3 0.7 all-gather.9.cloned.1.call-update
  8.1 0.7 all-gather.5.cloned.1.call-update
  8.8 0.5 all-gather.11.cloned.1.call-update
  9.4 1.6 convert_element_type.57
  11.0 21.7 %gather_fusion = bf16[1024,5120]{1,0:T(8,128)(2,1)} fusion(bf16[512,5120]{1,0:T(8,128)(2,1)} %param.13, s32[1024]{0:T(1024)S(1)} %bitcast_clamp_fusion), kind=kCustom, calls=%fused_computation | custom fusion | bytes 20975616 | tf_op jit(solution)/shard_map/jit(_take)/gather | solution.py:11
  32.7 11.0 %add_convert_fusion = bf16[8,128,5120]{2,1,0:T(8,128)(2,1)} fusion(f32[128,5120]{1,0:T(8,128)S(1)} %convert_element_type.57, bf16[8,128,5120]{2,1,0:T(8,128)(2,1)} %bitcast.28, pred[8,128]{1,0:T(8,128)(4,1)S(1)} %compare_and_fusion), kind=kLoop, calls=%fused_computation.7 | loop fusion | flops 20971520 | bytes 23593984 | tf_op jit(solution)/shard_map/convert_element_type | solution.py:14
  43.7 0.6 dynamic_slice.7
  44.3 0.6 iota_compare_fusion.1
  45.0 6.5 %fusion.1 = f32[8,128]{1,0:T(8,128)S(1)} fusion(bf16[8,128,5120]{2,1,0:T(8,128)(2,1)} %add_convert_fusion), kind=kLoop, calls=%fused_computation.4 | loop fusion | flops 15727616 | bytes 10489856 | tf_op jit(solution)/shard_map/reduce_sum | solution.py:16
  51.5 0.8 copy-done
  52.4 5.9 %fusion.3 = bf16[8,128,5120]{2,1,0:T(8,128)(2,1)} fusion(bf16[8,128,5120]{2,1,0:T(8,128)(2,1)S(1)} %copy-done, f32[5120]{0:T(1024)S(1)} %copy-done.3, f32[8,128]{1,0:T(8,128)S(1)} %add_rsqrt_fusion), kind=kLoop, calls=%fused_computation.6 | loop fusion | flops 20971520 | bytes 20996096 | tf_op jit(solution)/shard_map/convert_element_type | solution.py:17
  58.3 17.0 %all-gather.7.cloned.1.call-done = bf16[5120,640]{1,0:T(8,128)(2,1)} async-done(((bf16[320,640]{1,0:T(8,128)(2,1)}), bf16[5120,640]{1,0:T(8,128)(2,1)}) %all-gather.7.cloned.1.call-update) | async-done | bytes 6553616 | tf_op jit(solution)/shard_map/all_gather | solution.py:55
  75.3 12.9 %convolution_convert_fusion.3 = bf16[1024,640]{1,0:T(8,128)(2,1)S(1)} fusion(bf16[1024,5120]{1,0:T(8,128)(2,1)} %bitcast.30, bf16[5120,640]{1,0:T(8,128)(2,1)} %all-gather.7.cloned.1.call-done), kind=kOutput, calls=%fused_computation.16 | convolution fusion | flops 6711541760 | bytes 18350080 | tf_op jit(solution)/shard_map/dot_general | solution.py:54
  88.2 1.5 reshape.103
  89.7 49.9 %all-gather.9.cloned.1.call-done = bf16[5120,640]{1,0:T(8,128)(2,1)} async-done(((bf16[320,640]{1,0:T(8,128)(2,1)}), bf16[5120,640]{1,0:T(8,128)(2,1)}) %all-gather.9.cloned.1.call-update) | async-done | bytes 6553616 | tf_op jit(solution)/shard_map/all_gather | solution.py:58
  139.6 12.9 %convolution_convert_fusion.2 = bf16[1024,640]{1,0:T(8,128)(2,1)S(1)} fusion(bf16[1024,5120]{1,0:T(8,128)(2,1)} %bitcast.31, bf16[5120,640]{1,0:T(8,128)(2,1)} %all-gather.9.cloned.1.call-done), kind=kOutput, calls=%fused_computation.15 | convolution fusion | flops 6711541760 | bytes 18350080 | tf_op jit(solution)/shard_map/dot_general | solution.py:57
  152.5 2.5 reshape.104
  154.9 48.9 %all-gather.5.cloned.1.call-done = bf16[5120,640]{1,0:T(8,128)(2,1)} async-done(((bf16[320,640]{1,0:T(8,128)(2,1)}), bf16[5120,640]{1,0:T(8,128)(2,1)}) %all-gather.5.cloned.1.call-update) | async-done | bytes 6553616 | tf_op jit(solution)/shard_map/all_gather | solution.py:61
  203.9 12.9 %convolution_convert_fusion.4 = bf16[1024,640]{1,0:T(8,128)(2,1)S(1)} fusion(bf16[1024,5120]{1,0:T(8,128)(2,1)} %bitcast.32, bf16[5120,640]{1,0:T(8,128)(2,1)} %all-gather.5.cloned.1.call-done), kind=kOutput, calls=%fused_computation.17 | convolution fusion | flops 6711541760 | bytes 18350080 | tf_op jit(solution)/shard_map/dot_general | solution.py:60
  216.8 2.5 reshape.102
  219.3 2.6 fusion.8
  221.9 1.5 copy-done.1
  223.4 0.8 fusion.23
  224.4 3.1 fusion.5
  227.5 0.9 copy.30
  228.4 39.6 %all-gather.11.cloned.1.call-done = bf16[640,5120]{0,1:T(8,128)(2,1)} async-done(((bf16[640,320]{0,1:T(8,128)(2,1)}), bf16[640,5120]{0,1:T(8,128)(2,1)}) %all-gather.11.cloned.1.call-update) | async-done | bytes 6553616 | tf_op jit(solution)/shard_map/all_gather | solution.py:70
  268.0 13.7 %convolution_convert_fusion = bf16[1024,5120]{1,0:T(8,128)(2,1)} fusion(bf16[640,5120]{0,1:T(8,128)(2,1)} %all-gather.11.cloned.1.call-done, bf16[80,8,8,128]{3,2,1,0:T(8,128)(2,1)S(1)} %bitcast.34), kind=kOutput, calls=%fused_computation.8 | convolution fusion | flops 6716129280 | bytes 18350080 | tf_op jit(solution)/shard_map/dot_general | solution.py:69
  281.7 14.4 %copy.38 = bf16[1024,5120]{0,1:T(8,128)(2,1)} copy(bf16[1024,5120]{1,0:T(8,128)(2,1)} %convolution_convert_fusion) | data formatting | bytes 20971520
  296.2 61.6 %reduce-scatter.4.cloned.1.call-done = bf16[640,1024]{1,0:T(8,128)(2,1)} async-done(((bf16[5120,1024]{1,0:T(8,128)(2,1)}), bf16[640,1024]{1,0:T(8,128)(2,1)}) %reduce-scatter.4.cloned.1.call-update) | async-done | bytes 1310736
  357.7 1.7 copy.39
  359.4 2.8 multiply_convert_fusion
  (22 shorter events, 0.5 us)
Async XLA Ops:
  6.5 68.7 %all-gather.7.cloned.1.call-start = ((), (), s32[]{:S(2)}) async-start(), calls=%async_computation.2 | async-start | bytes 6963200 | tf_op jit(solution)/shard_map/all_gather | solution.py:55
  7.3 3.7 %copy-start.4 = (s32[8,128]{1,0:T(8,128)S(1)}, s32[8,128]{1,0:T(8,128)}, u32[]{:S(2)}) copy-start(s32[8,128]{1,0:T(8,128)} %param.10) | copy-start | bytes 12292
  7.3 132.3 %all-gather.9.cloned.1.call-start = ((), (), s32[]{:S(2)}) async-start(), calls=%async_computation.3 | async-start | bytes 6963200 | tf_op jit(solution)/shard_map/all_gather | solution.py:58
  8.0 195.8 %all-gather.5.cloned.1.call-start = ((), (), s32[]{:S(2)}) async-start(), calls=%async_computation.1 | async-start | bytes 6963200 | tf_op jit(solution)/shard_map/all_gather | solution.py:61
  8.8 259.3 %all-gather.11.cloned.1.call-start = ((), (), s32[]{:S(2)}) async-start(), calls=%async_computation.4 | async-start | bytes 6963200 | tf_op jit(solution)/shard_map/all_gather | solution.py:70
  9.3 348.4 %reduce-scatter.4.cloned.1.call-start = ((), (), s32[]{:S(2)}) async-start(), calls=%async_computation.5 | async-start | bytes 11796480
  32.7 11.0 %copy-start.6 = (s32[16]{0:T(128)S(1)}, s32[16]{0:T(128)}, u32[]{:S(2)}) copy-start(s32[16]{0:T(128)} %param.12) | copy-start | bytes 196
  32.7 12.2 %copy-start.5 = (s32[8]{0:T(128)S(1)}, s32[8]{0:T(128)}, u32[]{:S(2)}) copy-start(s32[8]{0:T(128)} %param.11) | copy-start | bytes 100
  32.7 18.8 %copy-start.3 = (f32[5120]{0:T(1024)S(1)}, f32[5120]{0:T(1024)}, u32[]{:S(2)}) copy-start(f32[5120]{0:T(1024)} %param.15) | copy-start | bytes 61444
  45.0 7.4 %copy-start = (bf16[8,128,5120]{2,1,0:T(8,128)(2,1)S(1)}, bf16[8,128,5120]{2,1,0:T(8,128)(2,1)}, u32[]{:S(2)}) copy-start(bf16[8,128,5120]{2,1,0:T(8,128)(2,1)} %add_convert_fusion) | copy-start | bytes 31457284
  221.9 1.5 copy-start.1
  221.9 2.5 copy-start.2
Sparse Core Ops, SparseCore 0:
  9.5 65.7 all-gather.6
  77.4 62.1 all-gather.8
  141.7 62.1 all-gather.4
  205.8 62.1 all-gather.10
  296.3 61.4 reduce-scatter.3
where the time goes:
time: 370 us; the launch traced here: 369 us
  waiting for transfers between devices  220 us (59%)
  matrix products  58.1 us (16%)
  local copies, waits for them, and re-layouts  48.2 us (13%)
  other arithmetic  29.3 us (8%)
  between operations  13.3 us (4%)
    unnamed x6, waiting for transfers between devices  64.2 us
    all_gather x1, waiting for transfers between devices, verify(): lax.all_gather(w_key, 'row', axis=0, tiled=True)  49.9 us
    all_gather x1, waiting for transfers between devices, verify(): lax.all_gather(w_value, 'row', axis=0, tiled=True)  48.9 us
    all_gather x1, waiting for transfers between devices, verify(): lax.all_gather(w_out, 'row', axis=1, tiled=True)  39.6 us
    gather x1, local copies, waits for them, and re-layouts, prepare(): jnp.take(embed_table, group_ids, axis=0).astype(jnp.float32)  21.7 us
    unnamed x16, local copies, waits for them, and re-layouts  18.6 us
    all_gather x1, waiting for transfers between devices, verify(): lax.all_gather(w_query, 'row', axis=0, tiled=True)  17 us
    dot_general x1, matrix products, verify(): jnp.dot(mixed, lax.all_gather(w_out, 'row', axis=1, tiled=True), preferre...  13.7 us
  transfers between devices with their start and end apart: 5, of which 5 were waited for; matrix products, arithmetic and copies ran while one was open for 27% of the time, Pallas kernels for 0%

commit v1 on v0

--- a/solution.py
+++ b/solution.py
@@ -1,9 +1,20 @@
+import functools
 import jax
 import jax.numpy as jnp
 from jax import lax
 from jax.sharding import PartitionSpec as P
 
 DH = 128
+
+
+def list_routes_all(sample, d_out):
+    taken_in = jax.lax.axis_size("row")
+    z_new = jnp.stack([sample] * taken_in, axis=0)
+    lower = jax.lax.all_to_all(z_new, "row", split_axis=0, concat_axis=0)
+    return jnp.concatenate(lower, axis=d_out)
+
+
+clear_types_up = functools.partial(list_routes_all, d_out=1)
 
 
 def prepare(group_ids, embed_table, position_table, norm_gain):
@@ -66,9 +77,7 @@
         values.astype(jnp.bfloat16),
         group_lengths,
     )
-    partial_value = jnp.dot(
-        mixed, lax.all_gather(w_out, "row", axis=1, tiled=True), preferred_element_type=jnp.float32
-    )
+    partial_value = jnp.dot(mixed, clear_types_up(w_out), preferred_element_type=jnp.float32)
     summed = lax.psum_scatter(
         partial_value.astype(jnp.bfloat16), "mp", scatter_dimension=1, tiled=True
     ).astype(jnp.float32)

time: 370 us -> 406 us (1.097)
  waiting for transfers between devices: 220 us -> 243 us
  starting transfers between devices: 0.15 us -> 8.59 us
  local copies, waits for them, and re-layouts: 48.2 us -> 52.7 us
    all_gather x1, waiting for transfers between devices: 17 us -> 79.1 us  [verify(): lax.all_gather(w_query, 'row', axis=0, tiled=True)]
    all_gather x1 -> x0, waiting for transfers between devices: 39.6 us -> none  [verify(): lax.all_gather(w_out, 'row', axis=1, tiled=True)]
    all_to_all x0 -> x1, starting transfers between devices: none -> 8.47 us  [list_routes_all(): lower = jax.lax.all_to_all(z_new, 'row', split_axis=0, concat_axis=0)]
    another operation x0 -> x1, local copies, waits for them, and re-layouts: none -> 4.45 us  [list_routes_all(): z_new = jnp.stack([sample] * taken_in, axis=0)]
    unnamed x6 -> x5, waiting for transfers between devices: 64.2 us -> 63.7 us
  transfers between devices with their start and end apart: 5 -> 5, of which waited for: 5 -> 4; matrix products, arithmetic and copies ran while one was open for 27% -> 26% of each run, Pallas kernels for 0% -> 0%
where the time goes in v1:
time: 406 us; the launch traced here: 405 us
  waiting for transfers between devices  243 us (60%)
  matrix products  58.3 us (14%)
  local copies, waits for them, and re-layouts  52.7 us (13%)
  other arithmetic  29.3 us (7%)
  between operations  13.3 us (3%)
  starting transfers between devices  8.59 us (2%)
    all_gather x1, waiting for transfers between devices, verify(): lax.all_gather(w_query, 'row', axis=0, tiled=True)  79.1 us
    unnamed x5, waiting for transfers between devices  63.7 us
    all_gather x1, waiting for transfers between devices, verify(): lax.all_gather(w_key, 'row', axis=0, tiled=True)  51.1 us
    all_gather x1, waiting for transfers between devices, verify(): lax.all_gather(w_value, 'row', axis=0, tiled=True)  48.9 us
    gather x1, local copies, waits for them, and re-layouts, prepare(): jnp.take(embed_table, group_ids, axis=0).astype(jnp.float32)  21.8 us
    unnamed x16, local copies, waits for them, and re-layouts  18.5 us
    dot_general x1, matrix products, verify(): jnp.dot(mixed, clear_types_up(w_out), preferred_element_type=jnp.float32)  14 us
    dot_general x1, matrix products, verify(): jnp.dot(flat, lax.all_gather(w_value, 'row', axis=0, tiled=True), preferr...  12.9 us
  transfers between devices with their start and end apart: 5, of which 4 were waited for; matrix products, arithmetic and copies ran while one was open for 26% of the time, Pallas kernels for 0%

profile of v1, /device:TPU:1, one launch (start us, length us, event | category | flops | bytes accessed | tf_op | source)
XLA Modules:
  0.0 404.8 jit_solution(9972556266043003958)
XLA Ops:
  6.5 0.7 all-gather.6.cloned.1.call-update
  7.3 0.7 all-gather.8.cloned.1.call-update
  8.1 0.7 all-gather.4.cloned.1.call-update
  8.7 4.4 %stack.2 = bf16[16,640,320]{1,2,0:T(8,128)(2,1)} broadcast(bf16[640,320]{0,1:T(8,128)(2,1)} %param.19), dimensions={1,2} | broadcast | bytes 6963200 | tf_op jit(solution)/shard_map/stack | solution.py:12
  13.2 8.5 %all-to-all-start = ((bf16[16,640,320]{1,2,0:T(8,128)(2,1)}), bf16[16,640,320]{1,2,0:T(8,128)(2,1)}, u32[]{:S(2)}, u32[]{:S(2)}) async-start(bf16[16,640,320]{1,2,0:T(8,128)(2,1)} %stack.2), calls=%async_computation | async-start | bytes 13107200 | tf_op jit(solution)/shard_map/all_to_all | solution.py:13
  21.7 1.6 convert_element_type.57
  23.4 21.8 %gather_fusion = bf16[1024,5120]{1,0:T(8,128)(2,1)} fusion(bf16[512,5120]{1,0:T(8,128)(2,1)} %param.13, s32[1024]{0:T(1024)S(1)} %bitcast_clamp_fusion), kind=kCustom, calls=%fused_computation | custom fusion | bytes 20975616 | tf_op jit(solution)/shard_map/jit(_take)/gather | solution.py:22
  45.3 11.0 %add_convert_fusion = bf16[8,128,5120]{2,1,0:T(8,128)(2,1)} fusion(f32[128,5120]{1,0:T(8,128)S(1)} %convert_element_type.57, bf16[8,128,5120]{2,1,0:T(8,128)(2,1)} %bitcast.31, pred[8,128]{1,0:T(8,128)(4,1)S(1)} %compare_and_fusion), kind=kLoop, calls=%fused_computation.7 | loop fusion | flops 20971520 | bytes 23593984 | tf_op jit(solution)/shard_map/convert_element_type | solution.py:25
  56.3 0.6 dynamic_slice.7
  56.9 6.3 %fusion.1 = f32[8,128]{1,0:T(8,128)S(1)} fusion(bf16[8,128,5120]{2,1,0:T(8,128)(2,1)} %add_convert_fusion), kind=kLoop, calls=%fused_computation.4 | loop fusion | flops 15727616 | bytes 10489856 | tf_op jit(solution)/shard_map/reduce_sum | solution.py:27
  63.2 0.7 copy-done
  63.9 5.9 %fusion.3 = bf16[8,128,5120]{2,1,0:T(8,128)(2,1)} fusion(bf16[8,128,5120]{2,1,0:T(8,128)(2,1)S(1)} %copy-done, f32[5120]{0:T(1024)S(1)} %copy-done.3, f32[8,128]{1,0:T(8,128)S(1)} %add_rsqrt_fusion), kind=kLoop, calls=%fused_computation.6 | loop fusion | flops 20971520 | bytes 20996096 | tf_op jit(solution)/shard_map/convert_element_type | solution.py:28
  69.9 0.6 iota_compare_fusion.1
  70.6 79.1 %all-gather.6.cloned.1.call-done = bf16[5120,640]{1,0:T(8,128)(2,1)} async-done(((bf16[320,640]{1,0:T(8,128)(2,1)}), bf16[5120,640]{1,0:T(8,128)(2,1)}) %all-gather.6.cloned.1.call-update) | async-done | bytes 6553616 | tf_op jit(solution)/shard_map/all_gather | solution.py:66
  149.7 12.9 %convolution_convert_fusion.3 = bf16[1024,640]{1,0:T(8,128)(2,1)S(1)} fusion(bf16[1024,5120]{1,0:T(8,128)(2,1)} %bitcast.33, bf16[5120,640]{1,0:T(8,128)(2,1)} %all-gather.6.cloned.1.call-done), kind=kOutput, calls=%fused_computation.16 | convolution fusion | flops 6711541760 | bytes 18350080 | tf_op jit(solution)/shard_map/dot_general | solution.py:65
  162.6 1.5 reshape.113
  164.1 51.1 %all-gather.8.cloned.1.call-done = bf16[5120,640]{1,0:T(8,128)(2,1)} async-done(((bf16[320,640]{1,0:T(8,128)(2,1)}), bf16[5120,640]{1,0:T(8,128)(2,1)}) %all-gather.8.cloned.1.call-update) | async-done | bytes 6553616 | tf_op jit(solution)/shard_map/all_gather | solution.py:69
  215.1 12.9 %convolution_convert_fusion.2 = bf16[1024,640]{1,0:T(8,128)(2,1)S(1)} fusion(bf16[1024,5120]{1,0:T(8,128)(2,1)} %bitcast.34, bf16[5120,640]{1,0:T(8,128)(2,1)} %all-gather.8.cloned.1.call-done), kind=kOutput, calls=%fused_computation.15 | convolution fusion | flops 6711541760 | bytes 18350080 | tf_op jit(solution)/shard_map/dot_general | solution.py:68
  228.0 2.5 reshape.114
  230.5 48.9 %all-gather.4.cloned.1.call-done = bf16[5120,640]{1,0:T(8,128)(2,1)} async-done(((bf16[320,640]{1,0:T(8,128)(2,1)}), bf16[5120,640]{1,0:T(8,128)(2,1)}) %all-gather.4.cloned.1.call-update) | async-done | bytes 6553616 | tf_op jit(solution)/shard_map/all_gather | solution.py:72
  279.4 12.9 %convolution_convert_fusion.4 = bf16[1024,640]{1,0:T(8,128)(2,1)S(1)} fusion(bf16[1024,5120]{1,0:T(8,128)(2,1)} %bitcast.35, bf16[5120,640]{1,0:T(8,128)(2,1)} %all-gather.4.cloned.1.call-done), kind=kOutput, calls=%fused_computation.17 | convolution fusion | flops 6711541760 | bytes 18350080 | tf_op jit(solution)/shard_map/dot_general | solution.py:71
  292.3 2.4 reshape.112
  294.8 2.6 fusion.8
  297.4 1.5 copy-done.1
  298.9 0.8 fusion.23
  299.9 3.0 fusion.5
  303.0 0.9 copy.31
  303.9 14.0 %convolution_convert_fusion = bf16[1024,5120]{1,0:T(8,128)(2,1)} fusion(bf16[640,5120]{0,1:T(8,128)(2,1)} %bitcast.6, bf16[80,8,8,128]{3,2,1,0:T(8,128)(2,1)S(1)} %bitcast.37), kind=kOutput, calls=%fused_computation.8 | convolution fusion | flops 6716129280 | bytes 18350080 | tf_op jit(solution)/shard_map/dot_general | solution.py:80
  317.8 14.4 %copy.39 = bf16[1024,5120]{0,1:T(8,128)(2,1)} copy(bf16[1024,5120]{1,0:T(8,128)(2,1)} %convolution_convert_fusion) | data formatting | bytes 20971520
  332.2 61.6 %reduce-scatter.4.cloned.1.call-done = bf16[640,1024]{1,0:T(8,128)(2,1)} async-done(((bf16[5120,1024]{1,0:T(8,128)(2,1)}), bf16[640,1024]{1,0:T(8,128)(2,1)}) %reduce-scatter.4.cloned.1.call-update) | async-done | bytes 1310736
  393.8 1.7 copy.40
  395.5 2.8 multiply_convert_fusion
  (22 shorter events, 0.4 us)
Async XLA Ops:
  6.5 143.1 %all-gather.6.cloned.1.call-start = ((), (), s32[]{:S(2)}) async-start(), calls=%async_computation.3 | async-start | bytes 6963200 | tf_op jit(solution)/shard_map/all_gather | solution.py:66
  7.3 207.9 %all-gather.8.cloned.1.call-start = ((), (), s32[]{:S(2)}) async-start(), calls=%async_computation.4 | async-start | bytes 6963200 | tf_op jit(solution)/shard_map/all_gather | solution.py:69
  8.0 271.4 %all-gather.4.cloned.1.call-start = ((), (), s32[]{:S(2)}) async-start(), calls=%async_computation.2 | async-start | bytes 6963200 | tf_op jit(solution)/shard_map/all_gather | solution.py:72
  13.2 290.7 %all-to-all-start = ((bf16[16,640,320]{1,2,0:T(8,128)(2,1)}), bf16[16,640,320]{1,2,0:T(8,128)(2,1)}, u32[]{:S(2)}, u32[]{:S(2)}) async-start(bf16[16,640,320]{1,2,0:T(8,128)(2,1)} %stack.2), calls=%async_computation | async-start | bytes 13107200 | tf_op jit(solution)/shard_map/all_to_all | solution.py:13
  21.7 1.7 copy-start.4
  21.7 372.1 %reduce-scatter.4.cloned.1.call-start = ((), (), s32[]{:S(2)}) async-start(), calls=%async_computation.5 | async-start | bytes 11796480
  45.2 11.0 %copy-start.6 = (s32[16]{0:T(128)S(1)}, s32[16]{0:T(128)}, u32[]{:S(2)}) copy-start(s32[16]{0:T(128)} %param.12) | copy-start | bytes 196
  45.2 17.9 %copy-start.3 = (f32[5120]{0:T(1024)S(1)}, f32[5120]{0:T(1024)}, u32[]{:S(2)}) copy-start(f32[5120]{0:T(1024)} %param.15) | copy-start | bytes 61444
  56.9 7.1 %copy-start = (bf16[8,128,5120]{2,1,0:T(8,128)(2,1)S(1)}, bf16[8,128,5120]{2,1,0:T(8,128)(2,1)}, u32[]{:S(2)}) copy-start(bf16[8,128,5120]{2,1,0:T(8,128)(2,1)} %add_convert_fusion) | copy-start | bytes 31457284
  63.9 6.6 %copy-start.5 = (s32[8]{0:T(128)S(1)}, s32[8]{0:T(128)}, u32[]{:S(2)}) copy-start(s32[8]{0:T(128)} %param.11) | copy-start | bytes 100
  297.4 1.5 copy-start.1
  297.4 2.5 copy-start.2
Sparse Core Ops, SparseCore 0:
  9.5 140.1 all-gather.5
  151.8 63.2 all-gather.7
  217.3 62.1 all-gather.3
  332.4 61.3 reduce-scatter.3
